TPU v7x, 32 devices: a whole 2x2x4 slice. The times are simulated.
32 devices in a mesh: cols: 4 (over y, x), rows: 8 (over z, core).
Axes of the slice: x: 2, y: 2, z: 4, core: 2. Of those that a mesh axis runs over, the one named last changes fastest.
Arguments:
- gradient: float32 [128, 8192], P('cols', 'rows'), may hold values from -100 to 100
- width_factor: float32 [128, 128], P(None, 'cols'), may hold values from -3 to 4, as said below
- diag_blocks: float32 [64, 128, 128], P('rows'), may hold values from -2 to 24, as said below
- jacobi_inverse: float32 [64, 128, 128], P('rows'), may hold values from -2 to 2, as said below
- coupling_tiles: bfloat16 [32, 128, 128], P('rows'), may hold values from -4 to 4, as said below
- tile_local: int32 [32], P('rows'), may hold values from 0 to 7
- tile_remote: int32 [32], P('rows'), may hold values from 0 to 63, as said below
- tile_count: int32 [8], P('rows'), may hold values from 0 to 3, as said below
Outputs:
- solution: float32 [128, 8192], P('cols', 'rows')
- residual: float32 [128, 8192], P('cols', 'rows')
Inputs may be any that keep to these rules, and one draw needn't show every extreme that they name: `tile_remote`: the live entries are the first tile_count entries of each device's list; they name distinct devices other than the owner, each at most once. For a live entry of device d naming block J of device e, device e has a live entry naming d's block with its tile the transpose. Pad entries hold valid indices. `tile_count`: at most 3 on one device, reached on some device. `coupling_tiles`: with diag_blocks and the live entries, M is symmetric positive definite. `diag_blocks`: symmetric positive definite tiles. `jacobi_inverse`: the inverses of diag_blocks, symmetric. `width_factor`: symmetric positive definite.
All inputs are finite; a program needn't handle non-finite values.
Results may differ from a plain program's by a relative error of at most 0.0085.
Values may be sent and summed in bfloat16 or wider, within the bound.
No kernel may reach another device: no remote copies, remote signals or barrier semaphores. Data moves between devices by JAX's collectives and lax.ppermute only.
A program may use at most 64 MiB of HBM per device.

v0:
```python
import jax
import jax.numpy as jnp
from jax import lax
from jax.sharding import PartitionSpec as P

BLOCK = 128
ITERS = 6
highest = lax.Precision.HIGHEST


def on_device(
    gradient,
    width_factor,
    diag_blocks,
    jacobi_inverse,
    coupling_tiles,
    tile_local,
    tile_remote,
    tile_count,
):
    width_dev, rows_dev = gradient.shape
    blocks_dev = diag_blocks.shape[0]
    slot_count = tile_local.shape[0]
    devices = lax.axis_size("rows")
    active_slot = jnp.arange(slot_count, dtype=jnp.int32) < tile_count[0]
    placing = (
        (tile_local[:, None] == jnp.arange(blocks_dev, dtype=jnp.int32)[None, :])
        & active_slot[:, None]
    ).astype(jnp.float32)
    owner_dev = tile_remote // blocks_dev
    matches = active_slot[:, None] & (
        owner_dev[:, None] == jnp.arange(devices, dtype=jnp.int32)[None, :]
    )
    request = jnp.sum(jnp.where(matches, (tile_remote % blocks_dev)[:, None], 0), axis=0)
    granted = lax.all_to_all(request, "rows", split_axis=0, concat_axis=0, tiled=True)

    def precondition(vector):
        blocks = vector.reshape(width_dev, blocks_dev, BLOCK)
        return jnp.einsum("enj,nji->eni", blocks, jacobi_inverse, precision=highest).reshape(
            width_dev, rows_dev
        )

    solution = jnp.zeros_like(gradient)
    residual = gradient
    precond_res = precondition(residual)
    direction = precond_res
    res_norm = lax.psum(jnp.sum(residual * precond_res), ("cols", "rows"))
    for iteration in range(ITERS):
        apply_blocks = direction.reshape(width_dev, blocks_dev, BLOCK)
        local_part = jnp.einsum("enj,nji->eni", apply_blocks, diag_blocks, precision=highest)
        rounded = direction.astype(jnp.bfloat16).reshape(width_dev, blocks_dev, BLOCK)
        incoming = lax.all_to_all(
            rounded[:, granted, :], "rows", split_axis=1, concat_axis=1, tiled=True
        )
        sources = incoming[:, owner_dev, :]
        products = jnp.einsum(
            "ekj,kji->eki", sources, coupling_tiles, preferred_element_type=jnp.float32
        )
        coupled = jnp.einsum("eki,kb->ebi", products, placing, precision=highest)
        summed = lax.psum(
            jnp.dot(
                width_factor, (local_part + coupled).reshape(width_dev, rows_dev), precision=highest
            ),
            "cols",
        )
        fisher_dir = lax.dynamic_slice_in_dim(
            summed, lax.axis_index("cols") * width_dev, width_dev, 0
        )
        precond_fisher = precondition(fisher_dir)
        curvature, cross_term, second_term = lax.psum(
            (
                jnp.sum(direction * fisher_dir),
                jnp.sum(fisher_dir * precond_res),
                jnp.sum(fisher_dir * precond_fisher),
            ),
            ("cols", "rows"),
        )
        step_size = res_norm / curvature
        solution = solution + step_size * direction
        residual = residual - step_size * fisher_dir
        if iteration + 1 < ITERS:
            precond_res = precond_res - step_size * precond_fisher
            next_norm = (
                res_norm - 2.0 * step_size * cross_term + step_size * step_size * second_term
            )
            direction = precond_res + next_norm / res_norm * direction
            res_norm = next_norm
    return (solution, residual)


def solution(mesh):
    placed = (
        P("cols", "rows"),
        P(None, "cols"),
        P("rows", None, None),
        P("rows", None, None),
        P("rows", None, None),
        P("rows"),
        P("rows"),
        P("rows"),
    )
    return jax.shard_map(
        on_device,
        mesh=mesh,
        in_specs=placed,
        out_specs=(P("cols", "rows"), P("cols", "rows")),
        check_vma=False,
    )
```

profile of v0, /device:TPU:0, one launch (start us, length us, event | category | flops | bytes accessed | tf_op | source)
XLA Modules:
  0.0 644.4 jit_solution(5383939424549361704)
XLA Ops:
  9.3 6.4 all-to-all-start
  17.2 4.0 all-to-all-done
  22.6 3.4 all-to-all-start.1
  26.1 5.7 all-to-all-done.1
  35.1 44.0 %all-reduce.12.cloned.1.call-done = f32[128,1024]{1,0:T(8,128)} async-done(((f32[128,1024]{1,0:T(8,128)}), f32[128,1024]{1,0:T(8,128)}) %all-reduce.12.cloned.1.call-update) | async-done | bytes 524304 | tf_op jit(solution)/shard_map/psum | solution.py:60
  80.5 1.6 fusion.25
  82.1 39.6 %all-reduce.4 = (f32[]{:T(128)}, f32[]{:T(128)}, f32[]{:T(128)}) all-reduce(f32[]{:T(128)} %get-tuple-element.24, f32[]{:T(128)} %get-tuple-element.23, f32[]{:T(128)} %get-tuple-element.22), channel_id=1, replica_groups=mesh['cols'=4,'rows'=8] {'cols','rows'}, use_global_device_ids=true, to_apply=%region_1.2 | all-reduce | flops 3 | bytes 24 | tf_op jit(solution)/shard_map/psum | solution.py:47
  126.0 9.3 %all_to_all.42 = bf16[32,8,128]{2,0,1:T(8,128)(2,1)S(1)} all-to-all(bf16[32,8,128]{2,0,1:T(8,128)(2,1)S(1)} %bitcast.343), channel_id=1, replica_groups=mesh['cols'=4,'rows'=8] {'rows'}, dimensions={1} | all-to-all | bytes 131072 | tf_op jit(solution)/shard_map/all_to_all | solution.py:52
  138.4 45.0 %all-reduce.14.cloned.1.call-done = f32[128,1024]{1,0:T(8,128)} async-done(((f32[128,1024]{1,0:T(8,128)}), f32[128,1024]{1,0:T(8,128)}) %all-reduce.14.cloned.1.call-update) | async-done | bytes 524304 | tf_op jit(solution)/shard_map/psum | solution.py:60
  185.7 39.6 %all-reduce.3 = (f32[]{:T(128)}, f32[]{:T(128)}, f32[]{:T(128)}) all-reduce(f32[]{:T(128)} %get-tuple-element.21, f32[]{:T(128)} %get-tuple-element.20, f32[]{:T(128)} %get-tuple-element.19), channel_id=1, replica_groups=mesh['cols'=4,'rows'=8] {'cols','rows'}, use_global_device_ids=true, to_apply=%region_10.11 | all-reduce | flops 3 | bytes 24 | tf_op jit(solution)/shard_map/psum | solution.py:70
  227.8 9.3 %all_to_all.43 = bf16[32,8,128]{2,0,1:T(8,128)(2,1)S(1)} all-to-all(bf16[32,8,128]{2,0,1:T(8,128)(2,1)S(1)} %bitcast.344), channel_id=1, replica_groups=mesh['cols'=4,'rows'=8] {'rows'}, dimensions={1} | all-to-all | bytes 131072 | tf_op jit(solution)/shard_map/all_to_all | solution.py:52
  240.2 45.0 %all-reduce.16.cloned.1.call-done = f32[128,1024]{1,0:T(8,128)} async-done(((f32[128,1024]{1,0:T(8,128)}), f32[128,1024]{1,0:T(8,128)}) %all-reduce.16.cloned.1.call-update) | async-done | bytes 524304 | tf_op jit(solution)/shard_map/psum | solution.py:60
  286.6 1.7 multiply_reduce_fusion.5
  288.3 39.6 %all-reduce.2 = (f32[]{:T(128)}, f32[]{:T(128)}, f32[]{:T(128)}) all-reduce(f32[]{:T(128)} %get-tuple-element.13, f32[]{:T(128)} %get-tuple-element.12, f32[]{:T(128)} %get-tuple-element.18), channel_id=1, replica_groups=mesh['cols'=4,'rows'=8] {'cols','rows'}, use_global_device_ids=true, to_apply=%region_17.18 | all-reduce | flops 3 | bytes 24 | tf_op jit(solution)/shard_map/psum | solution.py:70
  330.4 9.3 %all_to_all.44 = bf16[32,8,128]{2,0,1:T(8,128)(2,1)S(1)} all-to-all(bf16[32,8,128]{2,0,1:T(8,128)(2,1)S(1)} %bitcast.345), channel_id=1, replica_groups=mesh['cols'=4,'rows'=8] {'rows'}, dimensions={1} | all-to-all | bytes 131072 | tf_op jit(solution)/shard_map/all_to_all | solution.py:52
  342.8 45.0 %all-reduce.18.cloned.1.call-done = f32[128,1024]{1,0:T(8,128)} async-done(((f32[128,1024]{1,0:T(8,128)}), f32[128,1024]{1,0:T(8,128)}) %all-reduce.18.cloned.1.call-update) | async-done | bytes 524304 | tf_op jit(solution)/shard_map/psum | solution.py:60
  390.8 39.7 %all-reduce.1 = (f32[]{:T(128)}, f32[]{:T(128)}, f32[]{:T(128)}) all-reduce(f32[]{:T(128)} %get-tuple-element.17, f32[]{:T(128)} %get-tuple-element.16, f32[]{:T(128)} %get-tuple-element.15), channel_id=1, replica_groups=mesh['cols'=4,'rows'=8] {'cols','rows'}, use_global_device_ids=true, to_apply=%region_24.25 | all-reduce | flops 3 | bytes 24 | tf_op jit(solution)/shard_map/psum | solution.py:70
  433.2 9.3 %all_to_all.45 = bf16[32,8,128]{2,0,1:T(8,128)(2,1)S(1)} all-to-all(bf16[32,8,128]{2,0,1:T(8,128)(2,1)S(1)} %bitcast.346), channel_id=1, replica_groups=mesh['cols'=4,'rows'=8] {'rows'}, dimensions={1} | all-to-all | bytes 131072 | tf_op jit(solution)/shard_map/all_to_all | solution.py:52
  445.5 45.1 %all-reduce.20.cloned.1.call-done = f32[128,1024]{1,0:T(8,128)} async-done(((f32[128,1024]{1,0:T(8,128)}), f32[128,1024]{1,0:T(8,128)}) %all-reduce.20.cloned.1.call-update) | async-done | bytes 524304 | tf_op jit(solution)/shard_map/psum | solution.py:60
  493.6 39.6 %all-reduce = (f32[]{:T(128)}, f32[]{:T(128)}, f32[]{:T(128)}) all-reduce(f32[]{:T(128)} %get-tuple-element.11, f32[]{:T(128)} %get-tuple-element.10, f32[]{:T(128)} %get-tuple-element.14), channel_id=1, replica_groups=mesh['cols'=4,'rows'=8] {'cols','rows'}, use_global_device_ids=true, to_apply=%region_31.32 | all-reduce | flops 3 | bytes 24 | tf_op jit(solution)/shard_map/psum | solution.py:70
  535.8 9.3 %all_to_all.46 = bf16[32,8,128]{2,0,1:T(8,128)(2,1)S(1)} all-to-all(bf16[32,8,128]{2,0,1:T(8,128)(2,1)S(1)} %bitcast.342), channel_id=1, replica_groups=mesh['cols'=4,'rows'=8] {'rows'}, dimensions={1} | all-to-all | bytes 131072 | tf_op jit(solution)/shard_map/all_to_all | solution.py:52
  548.1 45.1 %all-reduce.22.cloned.1.call-done = f32[128,1024]{1,0:T(8,128)} async-done(((f32[128,1024]{1,0:T(8,128)}), f32[128,1024]{1,0:T(8,128)}) %all-reduce.22.cloned.1.call-update) | async-done | bytes 524304 | tf_op jit(solution)/shard_map/psum | solution.py:60
  594.7 39.5 %psum.178 = f32[]{:T(128)} all-reduce(f32[]{:T(128)} %multiply_reduce_fusion), channel_id=1, replica_groups=mesh['cols'=4,'rows'=8] {'cols','rows'}, use_global_device_ids=true, to_apply=%region_38.39 | all-reduce | flops 1 | bytes 8 | tf_op jit(solution)/shard_map/psum | solution.py:70
  635.7 1.9 multiply_subtract_fusion
  (89 shorter events, 39.3 us)
Async XLA Ops:
  7.2 8.5 %copy-start = (f32[8,128,128]{2,1,0:T(8,128)S(1)}, f32[8,128,128]{2,1,0:T(8,128)}, u32[]{:S(2)}) copy-start(f32[8,128,128]{2,1,0:T(8,128)} %param.11) | copy-start | bytes 1572868
  7.9 0.7 copy-start.6
  9.3 11.9 %all-to-all-start = ((s32[8,1,1]{2,1,0:T(1,128)}), s32[8,1,1]{2,1,0:T(1,128)S(1)}, u32[]{:S(2)}, u32[]{:S(2)}) async-start(s32[8,1,1]{2,1,0:T(1,128)} %copy.175), calls=%async_computation | async-start | bytes 8192 | tf_op jit(solution)/shard_map/all_to_all | solution.py:35
  15.7 10.4 %copy-start.7 = (s32[4]{0:T(128)S(1)}, s32[4]{0:T(128)}, u32[]{:S(2)}) copy-start(s32[4]{0:T(128)} %param.13) | copy-start | bytes 52
  15.7 16.7 %copy-start.2 = (bf16[4,128,128]{2,1,0:T(8,128)(2,1)S(1)}, bf16[4,128,128]{2,1,0:T(8,128)(2,1)}, u32[]{:S(2)}) copy-start(bf16[4,128,128]{2,1,0:T(8,128)(2,1)} %param.12) | copy-start | bytes 393220
  17.2 15.6 %copy-start.1 = (f32[8,128,128]{2,1,0:T(8,128)S(1)}, f32[8,128,128]{2,1,0:T(8,128)}, u32[]{:S(2)}) copy-start(f32[8,128,128]{2,1,0:T(8,128)} %param.10) | copy-start | bytes 1572868
  22.6 9.2 %all-to-all-start.1 = ((bf16[32,8,128]{2,0,1:T(8,128)(2,1)}), bf16[32,8,128]{2,0,1:T(8,128)(2,1)S(1)}, u32[]{:S(2)}, u32[]{:S(2)}) async-start(bf16[32,8,128]{2,0,1:T(8,128)(2,1)} %bitcast.5), calls=%async_computation.1 | async-start | bytes 131072 | tf_op jit(solution)/shard_map/all_to_all | solution.py:52
  26.0 53.0 %all-reduce.12.cloned.1.call-start = ((), (), s32[]{:S(2)}) async-start(), calls=%async_computation.7 | async-start | bytes 1048576 | tf_op jit(solution)/shard_map/psum | solution.py:60
  32.8 0.7 copy-start.4
  35.0 148.4 %all-reduce.14.cloned.1.call-start = ((), (), s32[]{:S(2)}) async-start(), calls=%async_computation.8 | async-start | bytes 1048576 | tf_op jit(solution)/shard_map/psum | solution.py:60
  35.1 45.4 %copy-start.3 = (f32[32,1024]{1,0:T(8,128)S(1)}, f32[32,1024]{1,0:T(8,128)}, u32[]{:S(2)}) copy-start(f32[32,1024]{1,0:T(8,128)} %param.8) | copy-start | bytes 393220
  138.3 146.9 %all-reduce.16.cloned.1.call-start = ((), (), s32[]{:S(2)}) async-start(), calls=%async_computation.9 | async-start | bytes 1048576 | tf_op jit(solution)/shard_map/psum | solution.py:60
  183.4 1.5 copy-start.5
  240.1 147.7 %all-reduce.18.cloned.1.call-start = ((), (), s32[]{:S(2)}) async-start(), calls=%async_computation.10 | async-start | bytes 1048576 | tf_op jit(solution)/shard_map/psum | solution.py:60
  342.7 147.9 %all-reduce.20.cloned.1.call-start = ((), (), s32[]{:S(2)}) async-start(), calls=%async_computation.11 | async-start | bytes 1048576 | tf_op jit(solution)/shard_map/psum | solution.py:60
  445.5 147.7 %all-reduce.22.cloned.1.call-start = ((), (), s32[]{:S(2)}) async-start(), calls=%async_computation.12 | async-start | bytes 1048576 | tf_op jit(solution)/shard_map/psum | solution.py:60
Sparse Core Ops, SparseCore 0:
  35.1 43.8 all-reduce.11
  138.4 44.9 all-reduce.13
  240.2 44.9 all-reduce.15
  342.8 44.8 all-reduce.17
  445.6 44.9 all-reduce.19
  548.2 44.9 all-reduce.21
where the time goes:
time: 646 us; the launch traced here: 644 us
  blocking collectives  284 us (44%)
  waiting for transfers between devices  279 us (43%)
  between operations  27.4 us (4%)
  matrix products  23.3 us (4%)
  other arithmetic  12 us (2%)
  starting transfers between devices  9.95 us (2%)
  local copies, waits for them, and re-layouts  8.86 us (1%)
    psum x6, waiting for transfers between devices, on_device(): lax.psum(jnp.dot(width_factor, (local_part + coupled).reshape(width_dev,...  269 us
    psum x5, blocking collectives, on_device(): lax.psum((jnp.sum(direction * fisher_dir), jnp.sum(fisher_dir * precond_r...  198 us
    all_to_all x5, blocking collectives, on_device(): lax.all_to_all(rounded[:, granted, :], 'rows', split_axis=1, concat_axis=...  46.4 us
    psum x1, blocking collectives, on_device(): res_norm = lax.psum(jnp.sum(residual * precond_res), ('cols', 'rows'))  39.6 us
  transfers between devices with their start and end apart: 8, of which 8 were waited for; matrix products, arithmetic and copies ran while one was open for 0% of the time, Pallas kernels for 0%

commit v1 on v0

--- a/solution.py
+++ b/solution.py
@@ -68,12 +68,15 @@
         )
         precond_fisher = precondition(fisher_dir)
         curvature, cross_term, second_term = lax.psum(
-            (
-                jnp.sum(direction * fisher_dir),
-                jnp.sum(fisher_dir * precond_res),
-                jnp.sum(fisher_dir * precond_fisher),
+            lax.psum(
+                (
+                    jnp.sum(direction * fisher_dir),
+                    jnp.sum(fisher_dir * precond_res),
+                    jnp.sum(fisher_dir * precond_fisher),
+                ),
+                "cols",
             ),
-            ("cols", "rows"),
+            "rows",
         )
         step_size = res_norm / curvature
         solution = solution + step_size * direction

time: 646 us -> 577 us (0.89)
  blocking collectives: 284 us -> 227 us
  waiting for transfers between devices: 279 us -> 268 us
    psum x5 -> x6, blocking collectives: 198 us -> 59.3 us  [on_device(): lax.psum((jnp.sum(direction * fisher_dir), jnp.sum(fisher_dir * precond_r...]
    psum x0 -> x6, blocking collectives: none -> 86.4 us  [on_device(): lax.psum(lax.psum((jnp.sum(direction * fisher_dir), jnp.sum(fisher_dir *...]
    psum x6, waiting for transfers between devices: 269 us -> 258 us  [on_device(): lax.psum(jnp.dot(width_factor, (local_part + coupled).reshape(width_dev,...]
where the time goes in v1:
time: 577 us; the launch traced here: 576 us
  waiting for transfers between devices  268 us (46%)
  blocking collectives  227 us (39%)
  between operations  27.4 us (5%)
  matrix products  23.3 us (4%)
  other arithmetic  11.9 us (2%)
  starting transfers between devices  9.96 us (2%)
  local copies, waits for them, and re-layouts  8.86 us (2%)
    psum x6, waiting for transfers between devices, on_device(): lax.psum(jnp.dot(width_factor, (local_part + coupled).reshape(width_dev,...  258 us
    psum x6, blocking collectives, on_device(): lax.psum(lax.psum((jnp.sum(direction * fisher_dir), jnp.sum(fisher_dir *...  86.4 us
    psum x6, blocking collectives, on_device(): lax.psum((jnp.sum(direction * fisher_dir), jnp.sum(fisher_dir * precond_r...  59.3 us
    all_to_all x5, blocking collectives, on_device(): lax.all_to_all(rounded[:, granted, :], 'rows', split_axis=1, concat_axis=...  41.5 us
    psum x1, blocking collectives, on_device(): res_norm = lax.psum(jnp.sum(residual * precond_res), ('cols', 'rows'))  39.5 us
  transfers between devices with their start and end apart: 8, of which 8 were waited for; matrix products, arithmetic and copies ran while one was open for 0% of the time, Pallas kernels for 0%

profile of v1, /device:TPU:0, one launch (start us, length us, event | category | flops | bytes accessed | tf_op | source)
XLA Modules:
  0.0 576.0 jit_solution(3620687472115969727)
XLA Ops:
  35.1 44.0 %all-reduce.17.cloned.1.call-done = f32[128,1024]{1,0:T(8,128)} async-done(((f32[128,1024]{1,0:T(8,128)}), f32[128,1024]{1,0:T(8,128)}) %all-reduce.17.cloned.1.call-update) | async-done | bytes 524304 | tf_op jit(solution)/shard_map/psum | solution.py:60
  82.1 39.5 %psum.265 = f32[]{:T(128)} all-reduce(f32[]{:T(128)} %get-tuple-element.24), channel_id=1, replica_groups=mesh['cols'=4,'rows'=8] {'cols','rows'}, use_global_device_ids=true, to_apply=%region_1.2 | all-reduce | flops 1 | bytes 8 | tf_op jit(solution)/shard_map/psum | solution.py:47
  121.6 11.4 %all-reduce.9 = (f32[]{:T(128)}, f32[]{:T(128)}) all-reduce(f32[]{:T(128)} %get-tuple-element.23, f32[]{:T(128)} %get-tuple-element.22), channel_id=1, replica_groups=mesh['cols'=4,'rows'=8] {'cols'}, use_global_device_ids=true, to_apply=%region_5.6 | all-reduce | flops 2 | bytes 16 | tf_op jit(solution)/shard_map/psum | solution.py:71
  133.1 14.2 %all-reduce.4 = (f32[]{:T(128)}, f32[]{:T(128)}) all-reduce(f32[]{:T(128)} %get-tuple-element.51, f32[]{:T(128)} %get-tuple-element.52), channel_id=1, replica_groups=mesh['cols'=4,'rows'=8] {'rows'}, use_global_device_ids=true, to_apply=%region_6.7 | all-reduce | flops 2 | bytes 16 | tf_op jit(solution)/shard_map/psum | solution.py:70
  151.6 8.3 %all_to_all.42 = bf16[32,8,128]{2,0,1:T(8,128)(2,1)S(1)} all-to-all(bf16[32,8,128]{2,0,1:T(8,128)(2,1)S(1)} %bitcast.343), channel_id=1, replica_groups=mesh['cols'=4,'rows'=8] {'rows'}, dimensions={1} | all-to-all | bytes 131072 | tf_op jit(solution)/shard_map/all_to_all | solution.py:52
  163.0 42.1 %all-reduce.19.cloned.1.call-done = f32[128,1024]{1,0:T(8,128)} async-done(((f32[128,1024]{1,0:T(8,128)}), f32[128,1024]{1,0:T(8,128)}) %all-reduce.19.cloned.1.call-update) | async-done | bytes 524304 | tf_op jit(solution)/shard_map/psum | solution.py:60
  207.2 9.6 %all-reduce.8 = (f32[]{:T(128)}, f32[]{:T(128)}, f32[]{:T(128)}) all-reduce(f32[]{:T(128)} %get-tuple-element.21, f32[]{:T(128)} %get-tuple-element.20, f32[]{:T(128)} %get-tuple-element.19), channel_id=1, replica_groups=mesh['cols'=4,'rows'=8] {'cols'}, use_global_device_ids=true, to_apply=%region_12.13 | all-reduce | flops 3 | bytes 24 | tf_op jit(solution)/shard_map/psum | solution.py:71
  216.9 14.4 %all-reduce.3 = (f32[]{:T(128)}, f32[]{:T(128)}, f32[]{:T(128)}) all-reduce(f32[]{:T(128)} %get-tuple-element.48, f32[]{:T(128)} %get-tuple-element.49, f32[]{:T(128)} %get-tuple-element.50), channel_id=1, replica_groups=mesh['cols'=4,'rows'=8] {'rows'}, use_global_device_ids=true, to_apply=%region_13.14 | all-reduce | flops 3 | bytes 24 | tf_op jit(solution)/shard_map/psum | solution.py:70
  233.9 8.3 %all_to_all.43 = bf16[32,8,128]{2,0,1:T(8,128)(2,1)S(1)} all-to-all(bf16[32,8,128]{2,0,1:T(8,128)(2,1)S(1)} %bitcast.344), channel_id=1, replica_groups=mesh['cols'=4,'rows'=8] {'rows'}, dimensions={1} | all-to-all | bytes 131072 | tf_op jit(solution)/shard_map/all_to_all | solution.py:52
  245.2 43.0 %all-reduce.21.cloned.1.call-done = f32[128,1024]{1,0:T(8,128)} async-done(((f32[128,1024]{1,0:T(8,128)}), f32[128,1024]{1,0:T(8,128)}) %all-reduce.21.cloned.1.call-update) | async-done | bytes 524304 | tf_op jit(solution)/shard_map/psum | solution.py:60
  291.2 9.6 %all-reduce.7 = (f32[]{:T(128)}, f32[]{:T(128)}, f32[]{:T(128)}) all-reduce(f32[]{:T(128)} %get-tuple-element.13, f32[]{:T(128)} %get-tuple-element.12, f32[]{:T(128)} %get-tuple-element.18), channel_id=1, replica_groups=mesh['cols'=4,'rows'=8] {'cols'}, use_global_device_ids=true, to_apply=%region_22.23 | all-reduce | flops 3 | bytes 24 | tf_op jit(solution)/shard_map/psum | solution.py:71
  300.9 14.4 %all-reduce.2 = (f32[]{:T(128)}, f32[]{:T(128)}, f32[]{:T(128)}) all-reduce(f32[]{:T(128)} %get-tuple-element.45, f32[]{:T(128)} %get-tuple-element.46, f32[]{:T(128)} %get-tuple-element.47), channel_id=1, replica_groups=mesh['cols'=4,'rows'=8] {'rows'}, use_global_device_ids=true, to_apply=%region_23.24 | all-reduce | flops 3 | bytes 24 | tf_op jit(solution)/shard_map/psum | solution.py:70
  317.8 8.3 %all_to_all.44 = bf16[32,8,128]{2,0,1:T(8,128)(2,1)S(1)} all-to-all(bf16[32,8,128]{2,0,1:T(8,128)(2,1)S(1)} %bitcast.345), channel_id=1, replica_groups=mesh['cols'=4,'rows'=8] {'rows'}, dimensions={1} | all-to-all | bytes 131072 | tf_op jit(solution)/shard_map/all_to_all | solution.py:52
  329.2 43.0 %all-reduce.23.cloned.1.call-done = f32[128,1024]{1,0:T(8,128)} async-done(((f32[128,1024]{1,0:T(8,128)}), f32[128,1024]{1,0:T(8,128)}) %all-reduce.23.cloned.1.call-update) | async-done | bytes 524304 | tf_op jit(solution)/shard_map/psum | solution.py:60
  375.3 9.6 %all-reduce.6 = (f32[]{:T(128)}, f32[]{:T(128)}, f32[]{:T(128)}) all-reduce(f32[]{:T(128)} %get-tuple-element.17, f32[]{:T(128)} %get-tuple-element.16, f32[]{:T(128)} %get-tuple-element.15), channel_id=1, replica_groups=mesh['cols'=4,'rows'=8] {'cols'}, use_global_device_ids=true, to_apply=%region_32.33 | all-reduce | flops 3 | bytes 24 | tf_op jit(solution)/shard_map/psum | solution.py:71
  384.8 14.5 %all-reduce.1 = (f32[]{:T(128)}, f32[]{:T(128)}, f32[]{:T(128)}) all-reduce(f32[]{:T(128)} %get-tuple-element.42, f32[]{:T(128)} %get-tuple-element.43, f32[]{:T(128)} %get-tuple-element.44), channel_id=1, replica_groups=mesh['cols'=4,'rows'=8] {'rows'}, use_global_device_ids=true, to_apply=%region_33.34 | all-reduce | flops 3 | bytes 24 | tf_op jit(solution)/shard_map/psum | solution.py:70
  402.0 8.3 %all_to_all.45 = bf16[32,8,128]{2,0,1:T(8,128)(2,1)S(1)} all-to-all(bf16[32,8,128]{2,0,1:T(8,128)(2,1)S(1)} %bitcast.346), channel_id=1, replica_groups=mesh['cols'=4,'rows'=8] {'rows'}, dimensions={1} | all-to-all | bytes 131072 | tf_op jit(solution)/shard_map/all_to_all | solution.py:52
  413.3 43.0 %all-reduce.25.cloned.1.call-done = f32[128,1024]{1,0:T(8,128)} async-done(((f32[128,1024]{1,0:T(8,128)}), f32[128,1024]{1,0:T(8,128)}) %all-reduce.25.cloned.1.call-update) | async-done | bytes 524304 | tf_op jit(solution)/shard_map/psum | solution.py:60
  459.3 9.6 %all-reduce.5 = (f32[]{:T(128)}, f32[]{:T(128)}, f32[]{:T(128)}) all-reduce(f32[]{:T(128)} %get-tuple-element.11, f32[]{:T(128)} %get-tuple-element.10, f32[]{:T(128)} %get-tuple-element.14), channel_id=1, replica_groups=mesh['cols'=4,'rows'=8] {'cols'}, use_global_device_ids=true, to_apply=%region_42.43 | all-reduce | flops 3 | bytes 24 | tf_op jit(solution)/shard_map/psum | solution.py:71
  468.9 14.5 %all-reduce = (f32[]{:T(128)}, f32[]{:T(128)}, f32[]{:T(128)}) all-reduce(f32[]{:T(128)} %get-tuple-element.39, f32[]{:T(128)} %get-tuple-element.40, f32[]{:T(128)} %get-tuple-element.41), channel_id=1, replica_groups=mesh['cols'=4,'rows'=8] {'rows'}, use_global_device_ids=true, to_apply=%region_43.44 | all-reduce | flops 3 | bytes 24 | tf_op jit(solution)/shard_map/psum | solution.py:70
  486.0 8.3 %all_to_all.46 = bf16[32,8,128]{2,0,1:T(8,128)(2,1)S(1)} all-to-all(bf16[32,8,128]{2,0,1:T(8,128)(2,1)S(1)} %bitcast.342), channel_id=1, replica_groups=mesh['cols'=4,'rows'=8] {'rows'}, dimensions={1} | all-to-all | bytes 131072 | tf_op jit(solution)/shard_map/all_to_all | solution.py:52
  497.2 43.0 %all-reduce.27.cloned.1.call-done = f32[128,1024]{1,0:T(8,128)} async-done(((f32[128,1024]{1,0:T(8,128)}), f32[128,1024]{1,0:T(8,128)}) %all-reduce.27.cloned.1.call-update) | async-done | bytes 524304 | tf_op jit(solution)/shard_map/psum | solution.py:60
  541.8 9.5 %psum.300 = f32[]{:T(128)} all-reduce(f32[]{:T(128)} %multiply_reduce_fusion), channel_id=1, replica_groups=mesh['cols'=4,'rows'=8] {'cols'}, use_global_device_ids=true, to_apply=%region_52.53 | all-reduce | flops 1 | bytes 8 | tf_op jit(solution)/shard_map/psum | solution.py:71
  551.4 14.4 %psum.301 = f32[]{:T(128)} all-reduce(f32[]{:T(128)} %psum.300), channel_id=1, replica_groups=mesh['cols'=4,'rows'=8] {'rows'}, use_global_device_ids=true, to_apply=%region_53.54 | all-reduce | flops 1 | bytes 8 | tf_op jit(solution)/shard_map/psum | solution.py:70
  (96 shorter events, 63.8 us)
Async XLA Ops:
  7.2 8.5 %copy-start = (f32[8,128,128]{2,1,0:T(8,128)S(1)}, f32[8,128,128]{2,1,0:T(8,128)}, u32[]{:S(2)}) copy-start(f32[8,128,128]{2,1,0:T(8,128)} %param.11) | copy-start | bytes 1572868
  7.9 0.7 copy-start.6
  9.3 11.9 %all-to-all-start = ((s32[8,1,1]{2,1,0:T(1,128)}), s32[8,1,1]{2,1,0:T(1,128)S(1)}, u32[]{:S(2)}, u32[]{:S(2)}) async-start(s32[8,1,1]{2,1,0:T(1,128)} %copy.175), calls=%async_computation | async-start | bytes 8192 | tf_op jit(solution)/shard_map/all_to_all | solution.py:35
  15.7 10.4 %copy-start.7 = (s32[4]{0:T(128)S(1)}, s32[4]{0:T(128)}, u32[]{:S(2)}) copy-start(s32[4]{0:T(128)} %param.13) | copy-start | bytes 52
  15.7 16.7 %copy-start.2 = (bf16[4,128,128]{2,1,0:T(8,128)(2,1)S(1)}, bf16[4,128,128]{2,1,0:T(8,128)(2,1)}, u32[]{:S(2)}) copy-start(bf16[4,128,128]{2,1,0:T(8,128)(2,1)} %param.12) | copy-start | bytes 393220
  17.2 15.6 %copy-start.1 = (f32[8,128,128]{2,1,0:T(8,128)S(1)}, f32[8,128,128]{2,1,0:T(8,128)}, u32[]{:S(2)}) copy-start(f32[8,128,128]{2,1,0:T(8,128)} %param.10) | copy-start | bytes 1572868
  22.6 9.2 %all-to-all-start.1 = ((bf16[32,8,128]{2,0,1:T(8,128)(2,1)}), bf16[32,8,128]{2,0,1:T(8,128)(2,1)S(1)}, u32[]{:S(2)}, u32[]{:S(2)}) async-start(bf16[32,8,128]{2,0,1:T(8,128)(2,1)} %bitcast.5), calls=%async_computation.1 | async-start | bytes 131072 | tf_op jit(solution)/shard_map/all_to_all | solution.py:52
  26.0 53.0 %all-reduce.17.cloned.1.call-start = ((), (), s32[]{:S(2)}) async-start(), calls=%async_computation.7 | async-start | bytes 1048576 | tf_op jit(solution)/shard_map/psum | solution.py:60
  32.8 0.7 copy-start.4
  35.0 170.0 %all-reduce.19.cloned.1.call-start = ((), (), s32[]{:S(2)}) async-start(), calls=%async_computation.8 | async-start | bytes 1048576 | tf_op jit(solution)/shard_map/psum | solution.py:60
  35.1 45.4 %copy-start.3 = (f32[32,1024]{1,0:T(8,128)S(1)}, f32[32,1024]{1,0:T(8,128)}, u32[]{:S(2)}) copy-start(f32[32,1024]{1,0:T(8,128)} %param.8) | copy-start | bytes 393220
  162.9 125.3 %all-reduce.21.cloned.1.call-start = ((), (), s32[]{:S(2)}) async-start(), calls=%async_computation.9 | async-start | bytes 1048576 | tf_op jit(solution)/shard_map/psum | solution.py:60
  205.0 1.5 copy-start.5
  245.2 127.0 %all-reduce.23.cloned.1.call-start = ((), (), s32[]{:S(2)}) async-start(), calls=%async_computation.10 | async-start | bytes 1048576 | tf_op jit(solution)/shard_map/psum | solution.py:60
  329.1 127.2 %all-reduce.25.cloned.1.call-start = ((), (), s32[]{:S(2)}) async-start(), calls=%async_computation.11 | async-start | bytes 1048576 | tf_op jit(solution)/shard_map/psum | solution.py:60
  413.2 127.0 %all-reduce.27.cloned.1.call-start = ((), (), s32[]{:S(2)}) async-start(), calls=%async_computation.12 | async-start | bytes 1048576 | tf_op jit(solution)/shard_map/psum | solution.py:60
Sparse Core Ops, SparseCore 0:
  35.1 43.8 all-reduce.16
  163.0 41.9 all-reduce.18
  245.3 42.8 all-reduce.20
  329.2 42.8 all-reduce.22
  413.4 42.8 all-reduce.24
  497.4 42.8 all-reduce.26
